TPU v7x, 32 devices: a whole 2x2x4 slice. The times are simulated.
32 devices in a mesh: groups: 2 (over y), wide: 8 (over z, x), head: 2 (over core).
Axes of the slice: x: 2, y: 2, z: 4, core: 2. Of those that a mesh axis runs over, the one named last changes fastest.
Arguments:
- tokens: bfloat16 [1024, 2048], P(('groups', 'wide'), 'head'), parts along dimension 0, may hold values from -6 to 6
- expert_ids: int32 [1024, 8], P(('groups', 'wide')), parts along dimension 0, may hold values from 0 to 7, as said below
- gate_scores: float32 [1024, 8], P(('groups', 'wide')), parts along dimension 0, may hold values from 0.25 to 1
- gate_proj: bfloat16 [8, 704, 2048], P('wide', 'head'), may hold values from -0.125 to 0.125
- up_proj: bfloat16 [8, 704, 2048], P('wide', 'head'), may hold values from -0.125 to 0.125
- down_proj: bfloat16 [8, 704, 2048], P('wide', 'head'), may hold values from -0.21875 to 0.21875
Outputs:
- mixed: bfloat16 [1024, 2048], P(('groups', 'wide'), 'head'), parts along dimension 0
There are 2 independent parts, one for each index of `groups`. A program takes and returns all parts, laid end to end along the dimension named above; an argument that names none is the same for every part. Nothing has to cross between parts.
Inputs may be any that keep to these rules, and one draw needn't show every extreme that they name: `expert_ids`: each row names 8 different experts. Within each aligned block of 64 rows at most 64 rows name the same expert, and in every draw one expert is named by exactly 64 rows of every such block.
All inputs are finite; a program needn't handle non-finite values.
Results may differ from a plain program's by a relative error of at most 0.01.
Values may be sent and summed in bfloat16 or wider, within the bound.
A program may use at most 64 MiB of HBM per device.

v0:
```python
import jax
import jax.numpy as jnp
from jax import lax
from jax.sharding import PartitionSpec as P


def local(tokens, expert_ids, gate_scores, gate_proj, up_proj, down_proj):
    experts = lax.axis_size("wide")
    tok_rows, top_count = expert_ids.shape
    ceiling = (tok_rows * top_count + experts - 1) // experts
    capacity = min(tok_rows, max(2, tok_rows // 8, 2 * ceiling))
    flat_ids = expert_ids.reshape(-1)
    expert_numbers = jnp.arange(experts, dtype=jnp.int32)
    onehot = (flat_ids[:, None] == expert_numbers[None, :]).astype(jnp.int32)
    earlier = jnp.cumsum(onehot, axis=0) - onehot
    slot_index = jnp.sum(earlier * onehot, axis=1)
    position = flat_ids * capacity + slot_index
    targets = jnp.arange(experts * capacity, dtype=jnp.int32)
    placing = jnp.any(
        position.reshape(tok_rows, top_count)[:, :, None] == targets[None, None, :], axis=1
    ).astype(jnp.bfloat16)
    w_gate = gate_proj[0]
    w_up = up_proj[0]
    w_down = down_proj[0]
    placed = lax.dot_general(
        placing, tokens, (((0,), (0,)), ((), ())), preferred_element_type=jnp.float32
    )
    outgoing = placed.astype(jnp.bfloat16).reshape(experts, capacity, tokens.shape[1])
    full_rows = lax.all_gather(
        lax.all_to_all(outgoing, "wide", split_axis=0, concat_axis=0, tiled=True),
        "head",
        axis=2,
        tiled=True,
    )
    src_count, item_count, feature_width = full_rows.shape
    stacked = full_rows.reshape(src_count * item_count, feature_width)
    gate_part = lax.dot_general(
        stacked, w_gate, (((1,), (1,)), ((), ())), preferred_element_type=jnp.float32
    )
    up_part = lax.dot_general(
        stacked, w_up, (((1,), (1,)), ((), ())), preferred_element_type=jnp.float32
    )
    hidden = (jax.nn.silu(gate_part) * up_part).astype(jnp.bfloat16)
    partial_value = jnp.dot(hidden, w_down, preferred_element_type=jnp.float32)
    partial_value = partial_value.reshape(src_count, item_count, feature_width)
    back = lax.psum_scatter(
        partial_value.astype(jnp.bfloat16), "head", scatter_dimension=2, tiled=True
    ).astype(jnp.float32)
    returned = lax.all_to_all(
        back.astype(jnp.bfloat16), "wide", split_axis=0, concat_axis=0, tiled=True
    ).astype(back.dtype)
    picked = returned.reshape(experts * capacity, returned.shape[2])[position]
    picked = picked.reshape(tok_rows, top_count, returned.shape[2])
    mixed = jnp.sum(gate_scores[:, :, None] * picked, axis=1)
    return mixed.astype(jnp.bfloat16)


def solution(mesh):
    return jax.shard_map(
        local,
        mesh=mesh,
        in_specs=(
            P(("groups", "wide"), "head"),
            P(("groups", "wide"), None),
            P(("groups", "wide"), None),
            P("wide", "head", None),
            P("wide", "head", None),
            P("wide", "head", None),
        ),
        out_specs=P(("groups", "wide"), "head"),
        check_vma=False,
    )
```

profile of v0, /device:TPU:0, one launch (start us, length us, event | category | flops | bytes accessed | tf_op | source)
XLA Modules:
  0.0 117.7 jit_solution(13483769979636147468)
XLA Ops:
  6.5 0.0 copy-start
  6.5 0.0 all-gather.2.cloned.1.call-start
  6.5 0.9 copy.16
  7.4 0.1 eq.42
  7.5 0.1 eq.38
  7.6 1.1 reduce-window.6
  8.8 0.2 slice_reduce_fusion
  9.0 0.1 fusion.14
  9.1 0.1 reduce_sum.23
  9.2 0.4 fusion.12
  9.6 1.4 %convolution_convert_fusion.1 = bf16[512,1024]{1,0:T(8,128)(2,1)S(1)} fusion(pred[64,512]{1,0:T(8,128)(4,1)S(1)} %fusion.12, bf16[64,1024]{1,0:T(8,128)(2,1)} %param.6), kind=kOutput, calls=%fused_computation.4 | convolution fusion | flops 67633152 | bytes 1212416 | tf_op jit(solution)/shard_map/dot_general | solution.py:25
  11.0 32.9 %all_to_all.10 = bf16[8,64,1024]{2,1,0:T(8,128)(2,1)} all-to-all(bf16[8,64,1024]{2,1,0:T(8,128)(2,1)S(1)} %bitcast.39), channel_id=1, replica_groups=mesh['groups'=2,'wide'=8,'head'=2] {'wide'}, dimensions={0} | all-to-all | bytes 2097152 | tf_op jit(solution)/shard_map/all_to_all | solution.py:30
  44.0 0.0 all-gather.2.cloned.1.call-update
  44.0 0.0 reduce-scatter.2.cloned.1.call-start
  44.0 9.7 %all-gather.2.cloned.1.call-done = bf16[8,64,2048]{2,1,0:T(8,128)(2,1)} async-done(((bf16[8,64,1024]{2,1,0:T(8,128)(2,1)}), bf16[8,64,2048]{2,1,0:T(8,128)(2,1)}) %all-gather.2.cloned.1.call-update) | async-done | bytes 2097168 | tf_op jit(solution)/shard_map/all_gather | solution.py:29
  53.8 3.1 %fusion.4 = f32[512,352]{0,1:T(8,128)S(1)} fusion(bf16[512,2048]{1,0:T(8,128)(2,1)} %bitcast.43, bf16[1,352,2048]{2,1,0:T(8,128)(2,1)} %param.9), kind=kOutput, calls=%fused_computation.8 | convolution fusion | flops 738197504 | bytes 4259840 | tf_op jit(solution)/shard_map/dot_general | solution.py:37
  56.8 0.0 copy-done.2
  56.9 0.0 copy-done.3
  56.9 1.0 fusion.9
  57.9 0.2 copy.19
  58.1 0.0 copy-done
  58.1 2.6 %convolution_convert_fusion = bf16[8,64,2048]{2,1,0:T(8,128)(2,1)} fusion(bf16[8,64,352]{2,1,0:T(8,128)(2,1)S(1)} %bitcast.40, bf16[1,352,2048]{2,1,0:T(8,128)(2,1)S(1)} %copy-done), kind=kOutput, calls=%fused_computation.1 | convolution fusion | flops 739246080 | bytes 3899392 | tf_op jit(solution)/shard_map/dot_general | solution.py:44
  60.7 0.0 reduce-scatter.2.cloned.1.call-update
  60.7 11.0 %reduce-scatter.2.cloned.1.call-done = bf16[8,64,1024]{2,1,0:T(8,128)(2,1)} async-done(((bf16[8,64,2048]{2,1,0:T(8,128)(2,1)}), bf16[8,64,1024]{2,1,0:T(8,128)(2,1)}) %reduce-scatter.2.cloned.1.call-update) | async-done | bytes 1048592 | tf_op jit(solution)/shard_map/reduce_scatter | solution.py:46
  71.7 5.9 %all-to-all-start.1 = ((bf16[8,64,1024]{2,1,0:T(8,128)(2,1)}), bf16[8,64,1024]{2,1,0:T(8,128)(2,1)}, u32[]{:S(2)}, u32[]{:S(2)}) async-start(bf16[8,64,1024]{2,1,0:T(8,128)(2,1)} %reduce-scatter.2.cloned.1.call-done), calls=%async_computation.2 | async-start | bytes 2097152 | tf_op jit(solution)/shard_map/all_to_all | solution.py:49
  77.5 0.1 mul.42
  77.6 0.0 copy-done.1
  77.6 0.7 copy.15
  78.3 25.4 %all-to-all-done.1 = bf16[8,64,1024]{2,1,0:T(8,128)(2,1)} async-done(((bf16[8,64,1024]{2,1,0:T(8,128)(2,1)}), bf16[8,64,1024]{2,1,0:T(8,128)(2,1)}, u32[]{:S(2)}, u32[]{:S(2)}) %all-to-all-start.1) | async-done | bytes 1048608 | tf_op jit(solution)/shard_map/all_to_all | solution.py:49
  103.8 1.5 %bitcast_convert_fusion = f32[512,1024]{1,0:T(8,128)S(1)} fusion(bf16[8,64,1024]{2,1,0:T(8,128)(2,1)} %all-to-all-done.1), kind=kLoop, calls=%fused_computation.12 | loop fusion | flops 524288 | bytes 3145728 | tf_op jit(solution)/shard_map/reshape | solution.py:52
  105.2 2.7 %gather_fusion = f32[512,1024]{1,0:T(8,128)} fusion(f32[512,1024]{1,0:T(8,128)S(1)} %bitcast_convert_fusion, s32[1024]{0:T(1024)S(1)} %pad_clamp_fusion), kind=kCustom, calls=%fused_computation | custom fusion | bytes 4196352 | tf_op jit(solution)/shard_map/gather | solution.py:52
  107.9 2.9 %fusion = bf16[64,1024]{1,0:T(8,128)(2,1)} fusion(f32[512,1024]{1,0:T(8,128)} %gather_fusion, f32[64,8]{1,0:T(8,128)} %copy.15), kind=kLoop, calls=%fused_computation.3 | loop fusion | flops 983040 | bytes 2230272 | tf_op jit(solution)/shard_map/reduce_sum | solution.py:54
  (9 shorter events, 0.1 us)
Async XLA Ops:
  6.5 51.5 %copy-start = (bf16[1,352,2048]{2,1,0:T(8,128)(2,1)S(1)}, bf16[1,352,2048]{2,1,0:T(8,128)(2,1)}, u32[]{:S(2)}) copy-start(bf16[1,352,2048]{2,1,0:T(8,128)(2,1)} %param.11) | copy-start | bytes 4325380
  6.5 47.2 %all-gather.2.cloned.1.call-start = ((), (), s32[]{:S(2)}) async-start(), calls=%async_computation.3 | async-start | bytes 3145728 | tf_op jit(solution)/shard_map/all_gather | solution.py:29
  44.0 27.7 %reduce-scatter.2.cloned.1.call-start = ((), (), s32[]{:S(2)}) async-start(), calls=%async_computation.4 | async-start | bytes 3145728 | tf_op jit(solution)/shard_map/reduce_scatter | solution.py:46
  53.7 3.1 %copy-start.2 = (bf16[8,64,2048]{2,1,0:T(8,128)(2,1)S(1)}, bf16[8,64,2048]{2,1,0:T(8,128)(2,1)}, u32[]{:S(2)}) copy-start(bf16[8,64,2048]{2,1,0:T(8,128)(2,1)} %all-gather.2.cloned.1.call-done) | copy-start | bytes 6291460
  53.7 3.1 %copy-start.3 = (bf16[1,352,2048]{2,1,0:T(8,128)(2,1)S(1)}, bf16[1,352,2048]{2,1,0:T(8,128)(2,1)}, u32[]{:S(2)}) copy-start(bf16[1,352,2048]{2,1,0:T(8,128)(2,1)} %param.10) | copy-start | bytes 4325380
  60.7 16.9 %copy-start.1 = (f32[64,8]{0,1:T(8,128)S(1)}, f32[64,8]{0,1:T(8,128)}, u32[]{:S(2)}) copy-start(f32[64,8]{0,1:T(8,128)} %param.8) | copy-start | bytes 6148
  71.7 32.1 %all-to-all-start.1 = ((bf16[8,64,1024]{2,1,0:T(8,128)(2,1)}), bf16[8,64,1024]{2,1,0:T(8,128)(2,1)}, u32[]{:S(2)}, u32[]{:S(2)}) async-start(bf16[8,64,1024]{2,1,0:T(8,128)(2,1)} %reduce-scatter.2.cloned.1.call-done), calls=%async_computation.2 | async-start | bytes 2097152 | tf_op jit(solution)/shard_map/all_to_all | solution.py:49
Sparse Core Ops, SparseCore 0:
  44.1 9.5 all-gather.1
  60.8 10.7 reduce-scatter.1
where the time goes:
time: 118 us
  waiting for transfers between devices  46.1 us (39%)
  blocking collectives  32.9 us (28%)
  between operations  13.5 us (11%)
  matrix products  8.06 us (7%)
  other arithmetic  6.06 us (5%)
  starting transfers between devices  5.91 us (5%)
  local copies, waits for them, and re-layouts  5.09 us (4%)
    all_to_all x1, blocking collectives, local(): lax.all_to_all(outgoing, 'wide', split_axis=0, concat_axis=0, tiled=True)  32.9 us
    all_to_all x1, waiting for transfers between devices, local(): lax.all_to_all(back.astype(jnp.bfloat16), 'wide', split_axis=0, concat_ax...  25.4 us
    reduce_scatter x1, waiting for transfers between devices, local(): lax.psum_scatter(partial_value.astype(jnp.bfloat16), 'head', scatter_dime...  11 us
    all_gather x1, waiting for transfers between devices, local(): lax.all_gather(lax.all_to_all(outgoing, 'wide', split_axis=0, concat_axis...  9.71 us
    all_to_all x1, starting transfers between devices, local(): lax.all_to_all(back.astype(jnp.bfloat16), 'wide', split_axis=0, concat_ax...  5.86 us
    dot_general x1, matrix products, local(): lax.dot_general(stacked, w_gate, (((1,), (1,)), ((), ())), preferred_elem...  3.08 us
    reduce_sum x1, other arithmetic, local(): mixed = jnp.sum(gate_scores[:, :, None] * picked, axis=1)  2.92 us
    gather x1, local copies, waits for them, and re-layouts, local(): picked = returned.reshape(experts * capacity, returned.shape[2])[position]  2.72 us
  transfers between devices with their start and end apart: 3, of which 3 were waited for; matrix products, arithmetic and copies ran while one was open for 1% of the time, Pallas kernels for 0%

commit v1 on v0

--- a/solution.py
+++ b/solution.py
@@ -1,10 +1,14 @@
+import functools
+
 import jax
 import jax.numpy as jnp
 from jax import lax
+from jax.experimental import pallas as pl
+from jax.experimental.pallas import tpu as pltpu
 from jax.sharding import PartitionSpec as P
 
 
-def local(tokens, expert_ids, gate_scores, gate_proj, up_proj, down_proj):
+def spread(tokens, expert_ids, gate_scores, gate_proj, up_proj, down_proj):
     experts = lax.axis_size("wide")
     tok_rows, top_count = expert_ids.shape
     ceiling = (tok_rows * top_count + experts - 1) // experts
@@ -55,6 +59,287 @@
     return mixed.astype(jnp.bfloat16)
 
 
+MESH = pl.DeviceIdType.MESH
+
+
+def kernel(
+    lines, tokens, ids, scores, gate_hbm, up_hbm, down_hbm, out,
+    w_gate, w_up, w_down, toks, wt_out, wt_in, hb_out, hb_in, own, xb_out, xb_in,
+    zb_out, zb_in, load_sem, swt, rwt, sz, rz, sx, rx, sh, rh, shb, rhb, sxb, rxb, szb, rzb,
+):
+    wide = lax.axis_index("wide")
+    head = lax.axis_index("head")
+    line = wide // 2
+    side = wide % 2
+    far_side = 1 - side
+    other = 1 - head
+    rows, width = tokens.shape
+    experts = 2 * lines
+
+    def at(line_to, side_to, head_to):
+        return {"wide": line_to * 2 + side_to, "head": head_to}
+
+    def rcopy(src, dst, ssem, rsem, target):
+        return pltpu.make_async_remote_copy(
+            src_ref=src, dst_ref=dst, send_sem=ssem, recv_sem=rsem,
+            device_id=target, device_id_type=MESH,
+        )
+
+    partner = at(line, side, other)
+    across = at(line, far_side, head)
+
+    loads = [
+        pltpu.make_async_copy(gate_hbm.at[0], w_gate, load_sem.at[0]),
+        pltpu.make_async_copy(up_hbm.at[0], w_up, load_sem.at[1]),
+        pltpu.make_async_copy(down_hbm.at[0], w_down, load_sem.at[2]),
+    ]
+    for c in loads:
+        c.start()
+
+    barrier = pltpu.get_barrier_semaphore()
+    for step in range(1, experts):
+        pl.semaphore_signal(
+            barrier, inc=1, device_id={"wide": (wide + step) % experts, "head": head},
+            device_id_type=MESH,
+        )
+    pl.semaphore_signal(barrier, inc=1, device_id=partner, device_id_type=MESH)
+
+    lanes = lax.broadcasted_iota(jnp.int32, (rows, 128), 1)
+    weight = jnp.zeros((rows, 128), jnp.float32)
+    for k in range(ids.shape[1]):
+        weight += jnp.where(lanes == ids[:, k : k + 1], scores[:, k : k + 1], 0.0)
+    padded = jnp.concatenate([weight, jnp.zeros((128 - rows, 128), jnp.float32)], axis=0)
+    turned = jnp.transpose(padded)[:experts]
+    wt_out[...] = turned
+    wt_in[wide] = turned
+    toks[line, side, head] = tokens[...]
+    pl.semaphore_wait(barrier, experts)
+
+    def z_send(step):
+        dest = (line + step) % lines
+        return rcopy(
+            tokens, toks.at[line, side, head], sz.at[dest], rz.at[line], at(dest, side, head)
+        )
+
+    def x_send(pos):
+        return rcopy(
+            toks.at[pos, side, head], toks.at[pos, side, head], sx.at[pos], rx.at[pos], across
+        )
+
+    def h_send(pos, sd):
+        return rcopy(
+            toks.at[pos, sd, head], toks.at[pos, sd, head], sh.at[pos, sd], rh.at[pos, sd], partner
+        )
+
+    def own_x():
+        return rcopy(tokens, toks.at[line, side, head], sx.at[line], rx.at[line], across)
+
+    def own_h():
+        return rcopy(
+            tokens, toks.at[line, side, head], sh.at[line, side], rh.at[line, side], partner
+        )
+
+    low = jnp.minimum(line, lines - 1 - line)
+    up_is_long = line < lines - 1 - line
+
+    def order(j):
+        d = (j + 1) // 2
+        near = line - d if j % 2 else line + d
+        return jnp.where(j <= 2 * low, near, jnp.where(up_is_long, j, lines - 1 - j))
+
+    places = [line] + [order(j) for j in range(1, lines)]
+
+    def z_to(dest):
+        return rcopy(
+            tokens, toks.at[line, side, head], sz.at[dest], rz.at[line], at(dest, side, head)
+        )
+
+    def wt_send(step):
+        return rcopy(
+            wt_out, wt_in.at[wide], swt.at[step], rwt.at[step],
+            {"wide": (wide + step) % experts, "head": head},
+        )
+
+    own_x().start()
+    for j in range(1, lines):
+        z_to(places[j]).start()
+    own_h().start()
+    for step in range(1, experts):
+        wt_send(step).start()
+
+    def z_arrive(j):
+        pos = places[j]
+        rcopy(tokens, toks.at[pos, side, head], sz.at[pos], rz.at[pos], across).wait_recv()
+        x_send(pos).start()
+        h_send(pos, side).start()
+
+    def x_arrive(j):
+        pos = places[j]
+        rcopy(
+            tokens, toks.at[pos, far_side, head], sx.at[pos], rx.at[pos], across
+        ).wait_recv()
+        h_send(pos, far_side).start()
+
+    mine = lax.broadcasted_iota(jnp.int32, (128, experts), 1) == wide
+
+    def column(sender):
+        return jnp.sum(
+            jnp.where(mine, jnp.transpose(wt_in[sender]), 0.0), axis=1, keepdims=True
+        )[:rows]
+
+    nt = (((1,), (1,)), ((), ()))
+
+    def compute(j):
+        pos = places[j]
+        for sd in range(2):
+            rcopy(
+                tokens, toks.at[pos, sd, other], sh.at[pos, sd], rh.at[pos, sd], partner
+            ).wait_recv()
+        if j == 0:
+            for step in range(1, experts):
+                wt_send(step).wait_recv()
+            loads[0].wait()
+            loads[1].wait()
+        gate = jnp.zeros((2 * rows, w_gate.shape[0]), jnp.float32)
+        up = gate
+        for hf in range(2):
+            block = toks[pos, :, hf].reshape(2 * rows, width)
+            span = slice(hf * width, (hf + 1) * width)
+            gate += lax.dot_general(block, w_gate[:, span], nt, preferred_element_type=jnp.float32)
+            up += lax.dot_general(block, w_up[:, span], nt, preferred_element_type=jnp.float32)
+        scale = jnp.concatenate([column(pos * 2), column(pos * 2 + 1)], axis=0)
+        hidden = (gate / (1.0 + jnp.exp(-gate)) * up * scale).astype(jnp.bfloat16)
+        if j == 0:
+            loads[2].wait()
+        theirs = pl.ds(pl.multiple_of(other * width, width), width)
+        part = jnp.dot(hidden, w_down[:, theirs], preferred_element_type=jnp.float32)
+        hb_out[pos] = part.astype(jnp.bfloat16).reshape(2, rows, width)
+        hb(pos).start()
+        ours = pl.ds(pl.multiple_of(head * width, width), width)
+        part = jnp.dot(hidden, w_down[:, ours], preferred_element_type=jnp.float32)
+        own[j] = part.reshape(2, rows, width)
+
+    def hb(pos):
+        return rcopy(hb_out.at[pos], hb_in.at[pos], shb.at[pos], rhb.at[pos], partner)
+
+    def xb(pos):
+        return rcopy(xb_out.at[pos], xb_in.at[pos], sxb.at[pos], rxb.at[pos], across)
+
+    def zb(pos):
+        return rcopy(
+            zb_out.at[pos], zb_in.at[line], szb.at[pos], rzb.at[line], at(pos, side, head)
+        )
+
+    def add_heads(j):
+        pos = places[j]
+        hb(pos).wait_recv()
+        xb_out[pos] = (
+            own[j, far_side] + hb_in[pos, far_side].astype(jnp.float32)
+        ).astype(jnp.bfloat16)
+        xb(pos).start()
+
+    def add_sides(j):
+        pos = places[j]
+        xb(pos).wait_recv()
+        total = (
+            own[j, side] + hb_in[pos, side].astype(jnp.float32)
+            + xb_in[pos].astype(jnp.float32)
+        )
+        if j == 0:
+            own[0, side] = total
+        else:
+            zb_out[pos] = total.astype(jnp.bfloat16)
+            zb(pos).start()
+
+    x_arrive(0)
+    for j in range(lines):
+        if j + 1 < lines:
+            z_arrive(j + 1)
+        compute(j)
+        if j + 1 < lines:
+            x_arrive(j + 1)
+        add_heads(j)
+        if j > 0:
+            add_sides(j - 1)
+    add_sides(lines - 1)
+    total = own[0, side]
+    for j in range(1, lines):
+        pos = places[j]
+        rcopy(
+            zb_out.at[pos], zb_in.at[pos], szb.at[pos], rzb.at[pos], across
+        ).wait_recv()
+        total += zb_in[pos].astype(jnp.float32)
+    out[...] = total.astype(jnp.bfloat16)
+
+    for step in range(1, experts):
+        wt_send(step).wait_send()
+    own_x().wait_send()
+    own_h().wait_send()
+    for j in range(1, lines):
+        pos = places[j]
+        z_to(pos).wait_send()
+        x_send(pos).wait_send()
+        h_send(pos, side).wait_send()
+        zb(pos).wait_send()
+    for j in range(lines):
+        pos = places[j]
+        h_send(pos, far_side).wait_send()
+        hb(pos).wait_send()
+        xb(pos).wait_send()
+
+
+def fused(tokens, expert_ids, gate_scores, gate_proj, up_proj, down_proj):
+    experts = lax.axis_size("wide")
+    lines = experts // 2
+    rows, width = tokens.shape
+    units, features = gate_proj.shape[1:]
+    bf16, f32 = jnp.bfloat16, jnp.float32
+    dma = pltpu.SemaphoreType.DMA
+    vmem = pl.BlockSpec(memory_space=pltpu.VMEM)
+    hbm = pl.BlockSpec(memory_space=pl.ANY)
+    return pl.pallas_call(
+        functools.partial(kernel, lines),
+        out_shape=jax.ShapeDtypeStruct((rows, width), bf16),
+        in_specs=[vmem, vmem, vmem, hbm, hbm, hbm],
+        out_specs=vmem,
+        scratch_shapes=[
+            pltpu.VMEM((units, features), bf16),
+            pltpu.VMEM((units, features), bf16),
+            pltpu.VMEM((units, features), bf16),
+            pltpu.VMEM((lines, 2, 2, rows, width), bf16),
+            pltpu.VMEM((experts, 128), f32),
+            pltpu.VMEM((experts, experts, 128), f32),
+            pltpu.VMEM((lines, 2, rows, width), bf16),
+            pltpu.VMEM((lines, 2, rows, width), bf16),
+            pltpu.VMEM((lines, 2, rows, width), f32),
+            pltpu.VMEM((lines, rows, width), bf16),
+            pltpu.VMEM((lines, rows, width), bf16),
+            pltpu.VMEM((lines, rows, width), bf16),
+            pltpu.VMEM((lines, rows, width), bf16),
+            dma((3,)),
+            dma((experts,)), dma((experts,)),
+            dma((lines,)), dma((lines,)),
+            dma((lines,)), dma((lines,)),
+            dma((lines, 2)), dma((lines, 2)),
+            dma((lines,)), dma((lines,)),
+            dma((lines,)), dma((lines,)),
+            dma((lines,)), dma((lines,)),
+        ],
+        compiler_params=pltpu.CompilerParams(
+            collective_id=0, has_side_effects=True, vmem_limit_bytes=48 * 1024 * 1024
+        ),
+    )(tokens, expert_ids, gate_scores, gate_proj, up_proj, down_proj)
+
+
+def local(tokens, expert_ids, gate_scores, gate_proj, up_proj, down_proj):
+    experts = lax.axis_size("wide")
+    rows, width = tokens.shape
+    everyone = expert_ids.shape[1] == experts and gate_proj.shape[0] == 1
+    if everyone and experts % 2 == 0 and rows <= 128 and gate_proj.shape[2] == 2 * width:
+        return fused(tokens, expert_ids, gate_scores, gate_proj, up_proj, down_proj)
+    return spread(tokens, expert_ids, gate_scores, gate_proj, up_proj, down_proj)
+
+
 def solution(mesh):
     return jax.shard_map(
         local,

time: 118 us -> 61.4 us (0.52)
  Pallas kernels: 0 us -> 53.9 us
  waiting for transfers between devices: 46.1 us -> 0 us
  blocking collectives: 32.9 us -> 0 us
  between operations: 13.5 us -> 0.01 us
  matrix products: 8.06 us -> 0 us
  other arithmetic: 6.06 us -> 0 us
  starting transfers between devices: 5.91 us -> 0 us
  local copies, waits for them, and re-layouts: 5.09 us -> 7.19 us
    pallas_call x0 -> x1, Pallas kernels: none -> 53.9 us  [fused(): pl.pallas_call(functools.partial(kernel, lines), out_shape=jax.ShapeDtype...]
    all_to_all x1 -> x0, blocking collectives: 32.9 us -> none  [local(): lax.all_to_all(outgoing, 'wide', split_axis=0, concat_axis=0, tiled=True)]
    all_to_all x1 -> x0, waiting for transfers between devices: 25.4 us -> none  [local(): lax.all_to_all(back.astype(jnp.bfloat16), 'wide', split_axis=0, concat_ax...]
    reduce_scatter x1 -> x0, waiting for transfers between devices: 11 us -> none  [local(): lax.psum_scatter(partial_value.astype(jnp.bfloat16), 'head', scatter_dime...]
    all_gather x1 -> x0, waiting for transfers between devices: 9.71 us -> none  [local(): lax.all_gather(lax.all_to_all(outgoing, 'wide', split_axis=0, concat_axis...]
    dot_general x4 -> x0, matrix products: 8.06 us -> none  [the longest x1 3.08 us: local(): lax.dot_general(stacked, w_gate, (((1,), (1,)), ((), ())), preferred_elem...]
    all_to_all x1 -> x0, starting transfers between devices: 5.86 us -> none  [local(): lax.all_to_all(back.astype(jnp.bfloat16), 'wide', split_axis=0, concat_ax...]
    unnamed x10 -> x11, local copies, waits for them, and re-layouts: 1.58 us -> 7.19 us
  transfers between devices with their start and end apart: 3 -> 0, of which waited for: 3 -> 0; matrix products, arithmetic and copies ran while one was open for 1% -> 0% of each run, Pallas kernels for 0% -> 0%
where the time goes in v1:
time: 61.4 us; the launch traced here: 61.1 us
  Pallas kernels  53.9 us (88%)
  local copies, waits for them, and re-layouts  7.19 us (12%)
    pallas_call x1, Pallas kernels, fused(): pl.pallas_call(functools.partial(kernel, lines), out_shape=jax.ShapeDtype...  53.9 us
    unnamed x11, local copies, waits for them, and re-layouts  7.19 us

profile of v1, /device:TPU:0, one launch (start us, length us, event | category | flops | bytes accessed | tf_op | source)
XLA Modules:
  0.0 61.1 jit_solution(14524112036822427319)
XLA Ops:
  0.0 0.8 %copy.7.ids = s32[64,8]{1,0:T(8,128)S(1)} copy(s32[64,8]{0,1:T(8,128)} %param.7) | data formatting | bytes 4096 | tf_op args[1]
  0.8 0.8 %copy.8.scores = f32[64,8]{1,0:T(8,128)S(1)} copy(f32[64,8]{0,1:T(8,128)} %param.8) | data formatting | bytes 4096 | tf_op args[2]
  1.5 0.0 copy-start
  1.5 1.4 %copy-done = bf16[1,352,2048]{2,1,0:T(8,128)(2,1)S(1)} copy-done((bf16[1,352,2048]{2,1,0:T(8,128)(2,1)S(1)}, bf16[1,352,2048]{2,1,0:T(8,128)(2,1)}, u32[]{:S(2)}) %copy-start) | copy-done | bytes 1441816
  2.9 0.0 copy-start.1
  2.9 1.4 %copy-done.1 = bf16[1,352,2048]{2,1,0:T(8,128)(2,1)S(1)} copy-done((bf16[1,352,2048]{2,1,0:T(8,128)(2,1)S(1)}, bf16[1,352,2048]{2,1,0:T(8,128)(2,1)}, u32[]{:S(2)}) %copy-start.1) | copy-done | bytes 1441816
  4.3 0.0 copy-start.2
  4.3 1.4 %copy-done.2 = bf16[1,352,2048]{2,1,0:T(8,128)(2,1)S(1)} copy-done((bf16[1,352,2048]{2,1,0:T(8,128)(2,1)S(1)}, bf16[1,352,2048]{2,1,0:T(8,128)(2,1)}, u32[]{:S(2)}) %copy-start.2) | copy-done | bytes 1441816
  5.6 0.0 copy-start.3
  5.6 0.9 %copy-done.3 = bf16[64,1024]{1,0:T(8,128)(2,1)S(1)} copy-done((bf16[64,1024]{1,0:T(8,128)(2,1)S(1)}, bf16[64,1024]{1,0:T(8,128)(2,1)}, u32[]{:S(2)}) %copy-start.3) | copy-done | bytes 131096
  6.5 53.9 %shard_map.64 = bf16[64,1024]{1,0:T(8,128)(2,1)S(1)} custom-call(bf16[64,1024]{1,0:T(8,128)(2,1)S(1)} %copy-done.3, s32[64,8]{1,0:T(8,128)S(1)} %copy.7.ids, f32[64,8]{1,0:T(8,128)S(1)} %copy.8.scores, bf16[1,352,2048]{2,1,0:T(8,128)(2,1)S(1)} %copy-done, bf16[1,352,2048]{2,1,0:T(8,128)(2,1)S(1)} %copy-done.1, bf16[1,352,2048]{2,1,0:T(8,128)(2,1)S(1)} %copy-done.2), custom_call_target="tpu_custom_call" | custom-call | tf_op jit(solution)/shard_map/pallas_call | solution.py:300
  60.5 0.7 %copy.10 = bf16[64,1024]{1,0:T(8,128)(2,1)} copy(bf16[64,1024]{1,0:T(8,128)(2,1)S(1)} %shard_map.64) | data formatting | bytes 262144
Async XLA Ops:
  1.5 1.4 %copy-start = (bf16[1,352,2048]{2,1,0:T(8,128)(2,1)S(1)}, bf16[1,352,2048]{2,1,0:T(8,128)(2,1)}, u32[]{:S(2)}) copy-start(bf16[1,352,2048]{2,1,0:T(8,128)(2,1)} %gate_hbm.1) | copy-start | bytes 4325380
  2.9 1.4 %copy-start.1 = (bf16[1,352,2048]{2,1,0:T(8,128)(2,1)S(1)}, bf16[1,352,2048]{2,1,0:T(8,128)(2,1)}, u32[]{:S(2)}) copy-start(bf16[1,352,2048]{2,1,0:T(8,128)(2,1)} %up_hbm.1) | copy-start | bytes 4325380
  4.3 1.4 %copy-start.2 = (bf16[1,352,2048]{2,1,0:T(8,128)(2,1)S(1)}, bf16[1,352,2048]{2,1,0:T(8,128)(2,1)}, u32[]{:S(2)}) copy-start(bf16[1,352,2048]{2,1,0:T(8,128)(2,1)} %down_hbm.1) | copy-start | bytes 4325380
  5.6 0.9 %copy-start.3 = (bf16[64,1024]{1,0:T(8,128)(2,1)S(1)}, bf16[64,1024]{1,0:T(8,128)(2,1)}, u32[]{:S(2)}) copy-start(bf16[64,1024]{1,0:T(8,128)(2,1)} %tokens.1) | copy-start | bytes 393220

commit v2 on v1

--- a/solution.py
+++ b/solution.py
@@ -63,8 +63,8 @@
 
 
 def kernel(
-    lines, tokens, ids, scores, gate_hbm, up_hbm, down_hbm, out,
-    w_gate, w_up, w_down, toks, wt_out, wt_in, hb_out, hb_in, own, xb_out, xb_in,
+    lines, tok_hbm, ids, scores, gate_hbm, up_hbm, down_hbm, out,
+    tokens, w_gate, w_up, w_down, toks, wt_out, wt_in, hb_out, hb_in, own, xb_out, xb_in,
     zb_out, zb_in, load_sem, swt, rwt, sz, rz, sx, rx, sh, rh, shb, rhb, sxb, rxb, szb, rzb,
 ):
     wide = lax.axis_index("wide")
@@ -88,6 +88,8 @@
     partner = at(line, side, other)
     across = at(line, far_side, head)
 
+    token_load = pltpu.make_async_copy(tok_hbm, tokens, load_sem.at[3])
+    token_load.start()
     loads = [
         pltpu.make_async_copy(gate_hbm.at[0], w_gate, load_sem.at[0]),
         pltpu.make_async_copy(up_hbm.at[0], w_up, load_sem.at[1]),
@@ -104,22 +106,16 @@
         )
     pl.semaphore_signal(barrier, inc=1, device_id=partner, device_id_type=MESH)
 
-    lanes = lax.broadcasted_iota(jnp.int32, (rows, 128), 1)
-    weight = jnp.zeros((rows, 128), jnp.float32)
-    for k in range(ids.shape[1]):
-        weight += jnp.where(lanes == ids[:, k : k + 1], scores[:, k : k + 1], 0.0)
-    padded = jnp.concatenate([weight, jnp.zeros((128 - rows, 128), jnp.float32)], axis=0)
-    turned = jnp.transpose(padded)[:experts]
+    named = lax.broadcasted_iota(jnp.int32, (experts, rows), 0)
+    turned = jnp.zeros((experts, rows), jnp.float32)
+    for k in range(ids.shape[0]):
+        turned += jnp.where(named == ids[k : k + 1], scores[k : k + 1], 0.0)
+    turned = jnp.concatenate([turned, jnp.zeros((experts, 128 - rows), jnp.float32)], axis=1)
     wt_out[...] = turned
     wt_in[wide] = turned
+    token_load.wait()
     toks[line, side, head] = tokens[...]
     pl.semaphore_wait(barrier, experts)
-
-    def z_send(step):
-        dest = (line + step) % lines
-        return rcopy(
-            tokens, toks.at[line, side, head], sz.at[dest], rz.at[line], at(dest, side, head)
-        )
 
     def x_send(pos):
         return rcopy(
@@ -296,13 +292,14 @@
     bf16, f32 = jnp.bfloat16, jnp.float32
     dma = pltpu.SemaphoreType.DMA
     vmem = pl.BlockSpec(memory_space=pltpu.VMEM)
-    hbm = pl.BlockSpec(memory_space=pl.ANY)
+    hbm = pl.BlockSpec(memory_space=pltpu.HBM)
     return pl.pallas_call(
         functools.partial(kernel, lines),
         out_shape=jax.ShapeDtypeStruct((rows, width), bf16),
-        in_specs=[vmem, vmem, vmem, hbm, hbm, hbm],
+        in_specs=[hbm, vmem, vmem, hbm, hbm, hbm],
         out_specs=vmem,
         scratch_shapes=[
+            pltpu.VMEM((rows, width), bf16),
             pltpu.VMEM((units, features), bf16),
             pltpu.VMEM((units, features), bf16),
             pltpu.VMEM((units, features), bf16),
@@ -316,7 +313,7 @@
             pltpu.VMEM((lines, rows, width), bf16),
             pltpu.VMEM((lines, rows, width), bf16),
             pltpu.VMEM((lines, rows, width), bf16),
-            dma((3,)),
+            dma((4,)),
             dma((experts,)), dma((experts,)),
             dma((lines,)), dma((lines,)),
             dma((lines,)), dma((lines,)),
@@ -326,9 +323,9 @@
             dma((lines,)), dma((lines,)),
         ],
         compiler_params=pltpu.CompilerParams(
-            collective_id=0, has_side_effects=True, vmem_limit_bytes=48 * 1024 * 1024
+            collective_id=0, has_side_effects=True, vmem_limit_bytes=63 * 1024 * 1024
         ),
-    )(tokens, expert_ids, gate_scores, gate_proj, up_proj, down_proj)
+    )(tokens, expert_ids.T, gate_scores.T, gate_proj, up_proj, down_proj)
 
 
 def local(tokens, expert_ids, gate_scores, gate_proj, up_proj, down_proj):

time: 61.4 us -> 56.2 us (0.915)
  local copies, waits for them, and re-layouts: 7.19 us -> 1.57 us
    unnamed x11 -> x1, local copies, waits for them, and re-layouts: 7.19 us -> 1.57 us
where the time goes in v2:
time: 56.2 us; the launch traced here: 56 us
  Pallas kernels  54.5 us (97%)
  local copies, waits for them, and re-layouts  1.57 us (3%)
    pallas_call x1, Pallas kernels, fused(): pl.pallas_call(functools.partial(kernel, lines), out_shape=jax.ShapeDtype...  54.5 us
    unnamed x1, local copies, waits for them, and re-layouts  1.57 us

profile of v2, /device:TPU:0, one launch (start us, length us, event | category | flops | bytes accessed | tf_op | source)
XLA Modules:
  0.0 56.0 jit_solution(10161047980529575685)
XLA Ops:
  0.0 54.5 %shard_map.64 = bf16[64,1024]{1,0:T(8,128)(2,1)} custom-call(bf16[64,1024]{1,0:T(8,128)(2,1)} %tok_hbm.1, s32[8,64]{1,0:T(8,128)} %bitcast.2, f32[8,64]{1,0:T(8,128)} %bitcast.3, bf16[1,352,2048]{2,1,0:T(8,128)(2,1)} %gate_hbm.1, bf16[1,352,2048]{2,1,0:T(8,128)(2,1)} %up_hbm.1, bf16[1,352,2048]{2,1,0:T(8,128)(2,1)} %down_hbm.1), custom_call_target="tpu_custom_call" | custom-call | tf_op jit(solution)/shard_map/pallas_call | solution.py:296
  54.5 1.6 %copy.8 = bf16[64,1024]{1,0:T(8,128)(2,1)} copy(bf16[64,1024]{1,0:T(8,128)(2,1)} %shard_map.64) | data formatting | bytes 262144

commit v3 on v2

--- a/solution.py
+++ b/solution.py
@@ -60,6 +60,7 @@
 
 
 MESH = pl.DeviceIdType.MESH
+CHUNKS = 2
 
 
 def kernel(
@@ -117,23 +118,32 @@
     toks[line, side, head] = tokens[...]
     pl.semaphore_wait(barrier, experts)
 
-    def x_send(pos):
+    chunk = rows // CHUNKS
+
+    def cut(ref, c):
+        return ref.at[pl.ds(c * chunk, chunk)]
+
+    def slot(pos, sd, hf, c):
+        return toks.at[pos, sd, hf, pl.ds(c * chunk, chunk)]
+
+    def z_send(pos, c, way):
+        src = cut(tokens, c) if pos is line else slot(pos, side, head, c)
+        to = line + 1 - 2 * way
         return rcopy(
-            toks.at[pos, side, head], toks.at[pos, side, head], sx.at[pos], rx.at[pos], across
-        )
-
-    def h_send(pos, sd):
-        return rcopy(
-            toks.at[pos, sd, head], toks.at[pos, sd, head], sh.at[pos, sd], rh.at[pos, sd], partner
-        )
-
-    def own_x():
-        return rcopy(tokens, toks.at[line, side, head], sx.at[line], rx.at[line], across)
-
-    def own_h():
-        return rcopy(
-            tokens, toks.at[line, side, head], sh.at[line, side], rh.at[line, side], partner
-        )
+            src, slot(pos, side, head, c), sz.at[pos, c, way], rz.at[pos, c], at(to, side, head)
+        )
+
+    def x_send(pos, c):
+        src = cut(tokens, c) if pos is line else slot(pos, side, head, c)
+        return rcopy(src, slot(pos, side, head, c), sx.at[pos, c], rx.at[pos, c], across)
+
+    def h_send(pos, far, c):
+        sd = far_side if far else side
+        src = cut(tokens, c) if pos is line and not far else slot(pos, sd, head, c)
+        return rcopy(src, slot(pos, sd, head, c), sh.at[pos, sd, c], rh.at[pos, sd, c], partner)
+
+    has_up = line < lines - 1
+    has_down = line > 0
 
     low = jnp.minimum(line, lines - 1 - line)
     up_is_long = line < lines - 1 - line
@@ -145,36 +155,48 @@
 
     places = [line] + [order(j) for j in range(1, lines)]
 
-    def z_to(dest):
-        return rcopy(
-            tokens, toks.at[line, side, head], sz.at[dest], rz.at[line], at(dest, side, head)
-        )
-
     def wt_send(step):
         return rcopy(
             wt_out, wt_in.at[wide], swt.at[step], rwt.at[step],
             {"wide": (wide + step) % experts, "head": head},
         )
 
-    own_x().start()
-    for j in range(1, lines):
-        z_to(places[j]).start()
-    own_h().start()
+    for c in range(CHUNKS):
+        x_send(line, c).start()
+
+        @pl.when(has_up)
+        def _():
+            z_send(line, c, 0).start()
+
+        @pl.when(has_down)
+        def _():
+            z_send(line, c, 1).start()
+
+        h_send(line, False, c).start()
     for step in range(1, experts):
         wt_send(step).start()
 
-    def z_arrive(j):
-        pos = places[j]
-        rcopy(tokens, toks.at[pos, side, head], sz.at[pos], rz.at[pos], across).wait_recv()
-        x_send(pos).start()
-        h_send(pos, side).start()
-
-    def x_arrive(j):
-        pos = places[j]
-        rcopy(
-            tokens, toks.at[pos, far_side, head], sx.at[pos], rx.at[pos], across
-        ).wait_recv()
-        h_send(pos, far_side).start()
+    def z_arrive(j, c):
+        pos = places[j]
+        dst = slot(pos, side, head, c)
+        rcopy(dst, dst, sz.at[pos, c, 0], rz.at[pos, c], across).wait_recv()
+
+        @pl.when(jnp.logical_and(pos < line, has_up))
+        def _():
+            z_send(pos, c, 0).start()
+
+        @pl.when(jnp.logical_and(pos > line, has_down))
+        def _():
+            z_send(pos, c, 1).start()
+
+        x_send(pos, c).start()
+        h_send(pos, False, c).start()
+
+    def x_arrive(j, c):
+        pos = places[j]
+        dst = slot(pos, far_side, head, c)
+        rcopy(dst, dst, sx.at[pos, c], rx.at[pos, c], across).wait_recv()
+        h_send(pos, True, c).start()
 
     mine = lax.broadcasted_iota(jnp.int32, (128, experts), 1) == wide
 
@@ -188,9 +210,9 @@
     def compute(j):
         pos = places[j]
         for sd in range(2):
-            rcopy(
-                tokens, toks.at[pos, sd, other], sh.at[pos, sd], rh.at[pos, sd], partner
-            ).wait_recv()
+            for c in range(CHUNKS):
+                dst = slot(pos, sd, other, c)
+                rcopy(dst, dst, sh.at[pos, sd, c], rh.at[pos, sd, c], partner).wait_recv()
         if j == 0:
             for step in range(1, experts):
                 wt_send(step).wait_recv()
@@ -247,17 +269,43 @@
             zb_out[pos] = total.astype(jnp.bfloat16)
             zb(pos).start()
 
-    x_arrive(0)
-    for j in range(lines):
-        if j + 1 < lines:
-            z_arrive(j + 1)
+    middle = low > 0
+    for c in range(CHUNKS):
+        x_arrive(0, c)
+        if lines > 1:
+            z_arrive(1, c)
+    for j in range(1, lines):
+        for c in range(CHUNKS):
+            if j == 1 and lines > 2:
+                z_arrive(2, c)
+            if 2 < j + 1 < lines:
+
+                @pl.when(jnp.logical_not(middle))
+                def _():
+                    z_arrive(j + 1, c)
+
+            x_arrive(j, c)
+            if 2 < j + 2 < lines:
+
+                @pl.when(middle)
+                def _():
+                    z_arrive(j + 2, c)
+
+        if j == 1:
+            compute(0)
         compute(j)
-        if j + 1 < lines:
-            x_arrive(j + 1)
-        add_heads(j)
-        if j > 0:
-            add_sides(j - 1)
-    add_sides(lines - 1)
+        if j > 1:
+            add_heads(j - 1)
+        if j > 2:
+            add_sides(j - 2)
+    if lines > 1:
+        add_heads(lines - 1)
+    add_heads(0)
+    if lines > 2:
+        add_sides(lines - 2)
+    if lines > 1:
+        add_sides(lines - 1)
+    add_sides(0)
     total = own[0, side]
     for j in range(1, lines):
         pos = places[j]
@@ -269,19 +317,25 @@
 
     for step in range(1, experts):
         wt_send(step).wait_send()
-    own_x().wait_send()
-    own_h().wait_send()
-    for j in range(1, lines):
-        pos = places[j]
-        z_to(pos).wait_send()
-        x_send(pos).wait_send()
-        h_send(pos, side).wait_send()
-        zb(pos).wait_send()
     for j in range(lines):
         pos = places[j]
-        h_send(pos, far_side).wait_send()
+        for c in range(CHUNKS):
+
+            @pl.when(jnp.logical_and(pos <= line, has_up))
+            def _():
+                z_send(pos, c, 0).wait_send()
+
+            @pl.when(jnp.logical_and(pos >= line, has_down))
+            def _():
+                z_send(pos, c, 1).wait_send()
+
+            x_send(pos, c).wait_send()
+            h_send(pos, False, c).wait_send()
+            h_send(pos, True, c).wait_send()
         hb(pos).wait_send()
         xb(pos).wait_send()
+        if j > 0:
+            zb(pos).wait_send()
 
 
 def fused(tokens, expert_ids, gate_scores, gate_proj, up_proj, down_proj):
@@ -315,9 +369,9 @@
             pltpu.VMEM((lines, rows, width), bf16),
             dma((4,)),
             dma((experts,)), dma((experts,)),
-            dma((lines,)), dma((lines,)),
-            dma((lines,)), dma((lines,)),
-            dma((lines, 2)), dma((lines, 2)),
+            dma((lines, CHUNKS, 2)), dma((lines, CHUNKS)),
+            dma((lines, CHUNKS)), dma((lines, CHUNKS)),
+            dma((lines, 2, CHUNKS)), dma((lines, 2, CHUNKS)),
             dma((lines,)), dma((lines,)),
             dma((lines,)), dma((lines,)),
             dma((lines,)), dma((lines,)),

time: 56.2 us -> 44.6 us (0.79)
  Pallas kernels: 54.5 us -> 42.8 us
    pallas_call x1, Pallas kernels: 54.5 us -> 42.8 us  [fused(): pl.pallas_call(functools.partial(kernel, lines), out_shape=jax.ShapeDtype...]
where the time goes in v3:
time: 44.6 us; the launch traced here: 44.4 us
  Pallas kernels  42.8 us (96%)
  local copies, waits for them, and re-layouts  1.57 us (4%)
    pallas_call x1, Pallas kernels, fused(): pl.pallas_call(functools.partial(kernel, lines), out_shape=jax.ShapeDtype...  42.8 us
    unnamed x1, local copies, waits for them, and re-layouts  1.57 us

profile of v3, /device:TPU:0, one launch (start us, length us, event | category | flops | bytes accessed | tf_op | source)
XLA Modules:
  0.0 44.4 jit_solution(14647625593990210806)
XLA Ops:
  0.0 42.8 %shard_map.64 = bf16[64,1024]{1,0:T(8,128)(2,1)} custom-call(bf16[64,1024]{1,0:T(8,128)(2,1)} %tok_hbm.1, s32[8,64]{1,0:T(8,128)} %bitcast.2, f32[8,64]{1,0:T(8,128)} %bitcast.3, bf16[1,352,2048]{2,1,0:T(8,128)(2,1)} %gate_hbm.1, bf16[1,352,2048]{2,1,0:T(8,128)(2,1)} %up_hbm.1, bf16[1,352,2048]{2,1,0:T(8,128)(2,1)} %down_hbm.1), custom_call_target="tpu_custom_call" | custom-call | tf_op jit(solution)/shard_map/pallas_call | solution.py:350
  42.8 1.6 %copy.8 = bf16[64,1024]{1,0:T(8,128)(2,1)} copy(bf16[64,1024]{1,0:T(8,128)(2,1)} %shard_map.64) | data formatting | bytes 262144

commit v4 on v3

--- a/solution.py
+++ b/solution.py
@@ -66,7 +66,7 @@
 def kernel(
     lines, tok_hbm, ids, scores, gate_hbm, up_hbm, down_hbm, out,
     tokens, w_gate, w_up, w_down, toks, wt_out, wt_in, hb_out, hb_in, own, xb_out, xb_in,
-    zb_out, zb_in, load_sem, swt, rwt, sz, rz, sx, rx, sh, rh, shb, rhb, sxb, rxb, szb, rzb,
+    zb_out, zb_in, load_sem, swz, rwz, swx, rwx, sz, rz, sx, rx, sh, rh, shb, rhb, sxb, rxb, szb, rzb,
 ):
     wide = lax.axis_index("wide")
     head = lax.axis_index("head")
@@ -100,11 +100,22 @@
         c.start()
 
     barrier = pltpu.get_barrier_semaphore()
-    for step in range(1, experts):
+    has_up = line < lines - 1
+    has_down = line > 0
+
+    @pl.when(has_up)
+    def _():
         pl.semaphore_signal(
-            barrier, inc=1, device_id={"wide": (wide + step) % experts, "head": head},
-            device_id_type=MESH,
-        )
+            barrier, inc=1, device_id=at(line + 1, side, head), device_id_type=MESH
+        )
+
+    @pl.when(has_down)
+    def _():
+        pl.semaphore_signal(
+            barrier, inc=1, device_id=at(line - 1, side, head), device_id_type=MESH
+        )
+
+    pl.semaphore_signal(barrier, inc=1, device_id=across, device_id_type=MESH)
     pl.semaphore_signal(barrier, inc=1, device_id=partner, device_id_type=MESH)
 
     named = lax.broadcasted_iota(jnp.int32, (experts, rows), 0)
@@ -116,7 +127,7 @@
     wt_in[wide] = turned
     token_load.wait()
     toks[line, side, head] = tokens[...]
-    pl.semaphore_wait(barrier, experts)
+    pl.semaphore_wait(barrier, 2 + jnp.where(has_up, 1, 0) + jnp.where(has_down, 1, 0))
 
     chunk = rows // CHUNKS
 
@@ -142,24 +153,37 @@
         src = cut(tokens, c) if pos is line and not far else slot(pos, sd, head, c)
         return rcopy(src, slot(pos, sd, head, c), sh.at[pos, sd, c], rh.at[pos, sd, c], partner)
 
-    has_up = line < lines - 1
-    has_down = line > 0
-
     low = jnp.minimum(line, lines - 1 - line)
     up_is_long = line < lines - 1 - line
+    toward = jnp.where(up_is_long, 1, -1)
 
     def order(j):
         d = (j + 1) // 2
-        near = line - d if j % 2 else line + d
+        near = line + toward * d if j % 2 else line - toward * d
         return jnp.where(j <= 2 * low, near, jnp.where(up_is_long, j, lines - 1 - j))
 
     places = [line] + [order(j) for j in range(1, lines)]
 
-    def wt_send(step):
+    def wt_z(pos, way):
+        src = wt_out if pos is line else wt_in.at[pos * 2 + side]
+        to = line + 1 - 2 * way
         return rcopy(
-            wt_out, wt_in.at[wide], swt.at[step], rwt.at[step],
-            {"wide": (wide + step) % experts, "head": head},
-        )
+            src, wt_in.at[pos * 2 + side], swz.at[pos, way], rwz.at[pos], at(to, side, head)
+        )
+
+    def wt_x(pos):
+        src = wt_out if pos is line else wt_in.at[pos * 2 + side]
+        return rcopy(src, wt_in.at[pos * 2 + side], swx.at[pos], rwx.at[pos], across)
+
+    wt_x(line).start()
+
+    @pl.when(has_up)
+    def _():
+        wt_z(line, 0).start()
+
+    @pl.when(has_down)
+    def _():
+        wt_z(line, 1).start()
 
     for c in range(CHUNKS):
         x_send(line, c).start()
@@ -173,11 +197,26 @@
             z_send(line, c, 1).start()
 
         h_send(line, False, c).start()
-    for step in range(1, experts):
-        wt_send(step).start()
+
+    def wt_arrive(j):
+        pos = places[j]
+        dst = wt_in.at[pos * 2 + side]
+        rcopy(dst, dst, swz.at[pos, 0], rwz.at[pos], across).wait_recv()
+
+        @pl.when(jnp.logical_and(pos < line, has_up))
+        def _():
+            wt_z(pos, 0).start()
+
+        @pl.when(jnp.logical_and(pos > line, has_down))
+        def _():
+            wt_z(pos, 1).start()
+
+        wt_x(pos).start()
 
     def z_arrive(j, c):
         pos = places[j]
+        if c == 0:
+            wt_arrive(j)
         dst = slot(pos, side, head, c)
         rcopy(dst, dst, sz.at[pos, c, 0], rz.at[pos, c], across).wait_recv()
 
@@ -214,10 +253,10 @@
                 dst = slot(pos, sd, other, c)
                 rcopy(dst, dst, sh.at[pos, sd, c], rh.at[pos, sd, c], partner).wait_recv()
         if j == 0:
-            for step in range(1, experts):
-                wt_send(step).wait_recv()
             loads[0].wait()
             loads[1].wait()
+        dst = wt_in.at[pos * 2 + far_side]
+        rcopy(dst, dst, swx.at[pos], rwx.at[pos], across).wait_recv()
         gate = jnp.zeros((2 * rows, w_gate.shape[0]), jnp.float32)
         up = gate
         for hf in range(2):
@@ -240,62 +279,68 @@
     def hb(pos):
         return rcopy(hb_out.at[pos], hb_in.at[pos], shb.at[pos], rhb.at[pos], partner)
 
-    def xb(pos):
-        return rcopy(xb_out.at[pos], xb_in.at[pos], sxb.at[pos], rxb.at[pos], across)
-
-    def zb(pos):
+    def xb(pos, c):
+        part = pl.ds(c * chunk, chunk)
         return rcopy(
-            zb_out.at[pos], zb_in.at[line], szb.at[pos], rzb.at[line], at(pos, side, head)
+            xb_out.at[pos, part], xb_in.at[pos, part], sxb.at[pos, c], rxb.at[pos, c], across
+        )
+
+    def zb(pos, c):
+        part = pl.ds(c * chunk, chunk)
+        return rcopy(
+            zb_out.at[pos, part], zb_in.at[line, part], szb.at[pos, c], rzb.at[line, c],
+            at(pos, side, head),
         )
 
     def add_heads(j):
         pos = places[j]
         hb(pos).wait_recv()
-        xb_out[pos] = (
-            own[j, far_side] + hb_in[pos, far_side].astype(jnp.float32)
-        ).astype(jnp.bfloat16)
-        xb(pos).start()
+        for c in range(CHUNKS):
+            part = slice(c * chunk, (c + 1) * chunk)
+            xb_out[pos, part] = (
+                own[j, far_side, part] + hb_in[pos, far_side, part].astype(jnp.float32)
+            ).astype(jnp.bfloat16)
+            xb(pos, c).start()
 
     def add_sides(j):
         pos = places[j]
-        xb(pos).wait_recv()
-        total = (
-            own[j, side] + hb_in[pos, side].astype(jnp.float32)
-            + xb_in[pos].astype(jnp.float32)
-        )
-        if j == 0:
-            own[0, side] = total
-        else:
-            zb_out[pos] = total.astype(jnp.bfloat16)
-            zb(pos).start()
+        for c in range(CHUNKS):
+            part = slice(c * chunk, (c + 1) * chunk)
+            xb(pos, c).wait_recv()
+            total = (
+                own[j, side, part] + hb_in[pos, side, part].astype(jnp.float32)
+                + xb_in[pos, part].astype(jnp.float32)
+            )
+            if j == 0:
+                own[0, side, part] = total
+            else:
+                zb_out[pos, part] = total.astype(jnp.bfloat16)
+                zb(pos, c).start()
 
     middle = low > 0
+
+    def z_arrive_if(wanted, j):
+        if j < lines:
+
+            @pl.when(wanted)
+            def _():
+                for c in range(CHUNKS):
+                    z_arrive(j, c)
+
     for c in range(CHUNKS):
         x_arrive(0, c)
         if lines > 1:
             z_arrive(1, c)
+    z_arrive_if(middle, 2)
+    compute(0)
     for j in range(1, lines):
-        for c in range(CHUNKS):
-            if j == 1 and lines > 2:
-                z_arrive(2, c)
-            if 2 < j + 1 < lines:
-
-                @pl.when(jnp.logical_not(middle))
-                def _():
-                    z_arrive(j + 1, c)
-
+        z_arrive_if(jnp.logical_not(middle), j + 1)
+        for c in range(CHUNKS):
             x_arrive(j, c)
-            if 2 < j + 2 < lines:
-
-                @pl.when(middle)
-                def _():
-                    z_arrive(j + 2, c)
-
-        if j == 1:
-            compute(0)
-        compute(j)
+        z_arrive_if(middle, j + 2)
         if j > 1:
             add_heads(j - 1)
+        compute(j)
         if j > 2:
             add_sides(j - 2)
     if lines > 1:
@@ -306,17 +351,18 @@
     if lines > 1:
         add_sides(lines - 1)
     add_sides(0)
-    total = own[0, side]
     for j in range(1, lines):
         pos = places[j]
-        rcopy(
-            zb_out.at[pos], zb_in.at[pos], szb.at[pos], rzb.at[pos], across
-        ).wait_recv()
-        total += zb_in[pos].astype(jnp.float32)
-    out[...] = total.astype(jnp.bfloat16)
-
-    for step in range(1, experts):
-        wt_send(step).wait_send()
+        for c in range(CHUNKS):
+            part = pl.ds(c * chunk, chunk)
+            dst = zb_in.at[pos, part]
+            rcopy(dst, dst, szb.at[pos, c], rzb.at[pos, c], across).wait_recv()
+            total = own[0, side, c * chunk : (c + 1) * chunk] + zb_in[pos, c * chunk : (c + 1) * chunk].astype(jnp.float32)
+            if j == lines - 1:
+                out[c * chunk : (c + 1) * chunk] = total.astype(jnp.bfloat16)
+            else:
+                own[0, side, c * chunk : (c + 1) * chunk] = total
+
     for j in range(lines):
         pos = places[j]
         for c in range(CHUNKS):
@@ -332,10 +378,20 @@
             x_send(pos, c).wait_send()
             h_send(pos, False, c).wait_send()
             h_send(pos, True, c).wait_send()
+        @pl.when(jnp.logical_and(pos <= line, has_up))
+        def _():
+            wt_z(pos, 0).wait_send()
+
+        @pl.when(jnp.logical_and(pos >= line, has_down))
+        def _():
+            wt_z(pos, 1).wait_send()
+
+        wt_x(pos).wait_send()
         hb(pos).wait_send()
-        xb(pos).wait_send()
-        if j > 0:
-            zb(pos).wait_send()
+        for c in range(CHUNKS):
+            xb(pos, c).wait_send()
+            if j > 0:
+                zb(pos, c).wait_send()
 
 
 def fused(tokens, expert_ids, gate_scores, gate_proj, up_proj, down_proj):
@@ -368,13 +424,14 @@
             pltpu.VMEM((lines, rows, width), bf16),
             pltpu.VMEM((lines, rows, width), bf16),
             dma((4,)),
-            dma((experts,)), dma((experts,)),
+            dma((lines, 2)), dma((lines,)),
+            dma((lines,)), dma((lines,)),
             dma((lines, CHUNKS, 2)), dma((lines, CHUNKS)),
             dma((lines, CHUNKS)), dma((lines, CHUNKS)),
             dma((lines, 2, CHUNKS)), dma((lines, 2, CHUNKS)),
             dma((lines,)), dma((lines,)),
-            dma((lines,)), dma((lines,)),
-            dma((lines,)), dma((lines,)),
+            dma((lines, CHUNKS)), dma((lines, CHUNKS)),
+            dma((lines, CHUNKS)), dma((lines, CHUNKS)),
         ],
         compiler_params=pltpu.CompilerParams(
             collective_id=0, has_side_effects=True, vmem_limit_bytes=63 * 1024 * 1024

time: 44.6 us -> 41 us (0.919)
  Pallas kernels: 42.8 us -> 39.2 us
    pallas_call x1, Pallas kernels: 42.8 us -> 39.2 us  [fused(): pl.pallas_call(functools.partial(kernel, lines), out_shape=jax.ShapeDtype...]
where the time goes in v4:
time: 41 us; the launch traced here: 40.8 us
  Pallas kernels  39.2 us (96%)
  local copies, waits for them, and re-layouts  1.57 us (4%)
    pallas_call x1, Pallas kernels, fused(): pl.pallas_call(functools.partial(kernel, lines), out_shape=jax.ShapeDtype...  39.2 us
    unnamed x1, local copies, waits for them, and re-layouts  1.57 us

profile of v4, /device:TPU:0, one launch (start us, length us, event | category | flops | bytes accessed | tf_op | source)
XLA Modules:
  0.0 40.8 jit_solution(17167536052827479257)
XLA Ops:
  0.0 39.2 %shard_map.64 = bf16[64,1024]{1,0:T(8,128)(2,1)} custom-call(bf16[64,1024]{1,0:T(8,128)(2,1)} %tok_hbm.1, s32[8,64]{1,0:T(8,128)} %bitcast.2, f32[8,64]{1,0:T(8,128)} %bitcast.3, bf16[1,352,2048]{2,1,0:T(8,128)(2,1)} %gate_hbm.1, bf16[1,352,2048]{2,1,0:T(8,128)(2,1)} %up_hbm.1, bf16[1,352,2048]{2,1,0:T(8,128)(2,1)} %down_hbm.1), custom_call_target="tpu_custom_call" | custom-call | tf_op jit(solution)/shard_map/pallas_call | solution.py:406
  39.2 1.6 %copy.8 = bf16[64,1024]{1,0:T(8,128)(2,1)} copy(bf16[64,1024]{1,0:T(8,128)(2,1)} %shard_map.64) | data formatting | bytes 262144

commit v5 on v4

--- a/solution.py
+++ b/solution.py
@@ -341,11 +341,11 @@
         if j > 1:
             add_heads(j - 1)
         compute(j)
-        if j > 2:
-            add_sides(j - 2)
     if lines > 1:
         add_heads(lines - 1)
     add_heads(0)
+    for j in range(1, lines - 2):
+        add_sides(j)
     if lines > 2:
         add_sides(lines - 2)
     if lines > 1:

time: 41 us -> 40.9 us (level)
  no operation moved by 1% of the time
where the time goes in v5:
time: 40.9 us; the launch traced here: 40.7 us
  Pallas kernels  39.1 us (96%)
  local copies, waits for them, and re-layouts  1.57 us (4%)
    pallas_call x1, Pallas kernels, fused(): pl.pallas_call(functools.partial(kernel, lines), out_shape=jax.ShapeDtype...  39.1 us
    unnamed x1, local copies, waits for them, and re-layouts  1.57 us

profile of v5, /device:TPU:0, one launch (start us, length us, event | category | flops | bytes accessed | tf_op | source)
XLA Modules:
  0.0 40.7 jit_solution(1024587830880624195)
XLA Ops:
  0.0 39.1 %shard_map.64 = bf16[64,1024]{1,0:T(8,128)(2,1)} custom-call(bf16[64,1024]{1,0:T(8,128)(2,1)} %tok_hbm.1, s32[8,64]{1,0:T(8,128)} %bitcast.2, f32[8,64]{1,0:T(8,128)} %bitcast.3, bf16[1,352,2048]{2,1,0:T(8,128)(2,1)} %gate_hbm.1, bf16[1,352,2048]{2,1,0:T(8,128)(2,1)} %up_hbm.1, bf16[1,352,2048]{2,1,0:T(8,128)(2,1)} %down_hbm.1), custom_call_target="tpu_custom_call" | custom-call | tf_op jit(solution)/shard_map/pallas_call | solution.py:406
  39.1 1.6 %copy.8 = bf16[64,1024]{1,0:T(8,128)(2,1)} copy(bf16[64,1024]{1,0:T(8,128)(2,1)} %shard_map.64) | data formatting | bytes 262144
